TPU v7x, 32 devices: a whole 2x2x4 slice. The times are simulated.
32 devices in a mesh: rve: 2 (over x), sub: 16 (over z, y, core).
Axes of the slice: x: 2, y: 2, z: 4, core: 2. Of those that a mesh axis runs over, the one named last changes fastest.
Arguments:
- condensed: float32 [49152, 1536], P(('rve', 'sub')), parts along dimension 0, may hold values from -0.15625 to 0.15625
- eigen_loads: float32 [49152, 128], P(('rve', 'sub')), parts along dimension 0, may hold values from -6 to 6
- coarse_inverse: float32 [1536, 768], P(('rve', 'sub')), parts along dimension 0, may hold values from -0.21875 to 0.21875
- face_rows: int32 [16, 2, 128], P('sub'), may hold values from 0 to 1535, as said below
- primal_rows: int32 [16, 96], P('sub'), may hold values from 0 to 1535, as said below
- primal_slot: int32 [16, 96], P('sub'), may hold values from 0 to 95, each once within a row
Outputs:
- displaced: float32 [49152, 128], P(('rve', 'sub')), parts along dimension 0
- multipliers: float32 [4096, 128], P(('rve', 'sub')), parts along dimension 0
There are 2 independent parts, one for each index of `rve`. A program takes and returns all parts, laid end to end along the dimension named above; an argument that names none is the same for every part. Nothing has to cross between parts.
Inputs may be any that keep to these rules, and one draw needn't show every extreme that they name: `face_rows`: in each subdomain the 128 left-face rows, the 128 right-face rows and the 96 primal rows in primal_rows are all distinct. `primal_rows`: distinct from that subdomain's face rows.
All inputs are finite; a program needn't handle non-finite values.
Results may differ from a plain program's by a relative error of at most 0.0001.
Values sent between devices are 32-bit elements; how exact they have to be, the bound alone decides.
A program may use at most 64 MiB of HBM per device.

v0:
```python
import jax
import jax.numpy as jnp
from jax import lax
from jax.sharding import PartitionSpec as P

ITERS = 3


DAMPING = 0.5


def passed_along(value, axis, steps):
    count = lax.axis_size(axis)
    pairs = [(source, (source + steps) % count) for source in range(count)]
    return lax.ppermute(value, axis, pairs)


def local(condensed, eigen_loads, coarse_inverse, face_rows, primal_rows, primal_slot):
    columns = eigen_loads.shape[1]
    owned = coarse_inverse.shape[0]
    width = face_rows.shape[2]
    left_rows = face_rows[0, 0]
    right_rows = face_rows[0, 1]
    prim_rows = primal_rows[0]
    slots = primal_slot[0]
    prolong = condensed[:, prim_rows]
    multipliers = jnp.zeros((width, columns), jnp.float32)
    previous = jnp.zeros((width, columns), jnp.float32)
    displaced = eigen_loads
    for step in range(ITERS):
        loads = eigen_loads.at[right_rows].add(-multipliers).at[left_rows].add(previous)
        displaced = jnp.dot(
            condensed, loads, precision=lax.Precision.HIGHEST, preferred_element_type=jnp.float32
        )
        slotted = jnp.zeros((2 * owned, columns), jnp.float32).at[slots].set(displaced[prim_rows])
        extended = jnp.concatenate([coarse_inverse, coarse_inverse[:, :owned]], axis=1)
        piece = lax.all_gather(slotted, "sub", axis=0, tiled=True)
        count = piece.shape[0] // (2 * owned)
        pieces = piece.reshape(count, 2, owned, columns)
        own_part = pieces[:, 0].reshape(count * owned, columns)
        sent_part = pieces[:, 1].reshape(count * owned, columns)
        next_cols = lax.dynamic_slice_in_dim(extended, owned, count * owned, 1)
        total = jnp.dot(
            coarse_inverse,
            own_part,
            precision=lax.Precision.HIGHEST,
            preferred_element_type=jnp.float32,
        )
        coarse_sol = total + jnp.dot(
            next_cols,
            sent_part,
            precision=lax.Precision.HIGHEST,
            preferred_element_type=jnp.float32,
        )
        coarse_next = passed_along(coarse_sol, "sub", -1)
        paired = jnp.concatenate([coarse_sol, coarse_next], axis=0)
        displaced = displaced - jnp.dot(
            prolong,
            paired[slots],
            precision=lax.Precision.HIGHEST,
            preferred_element_type=jnp.float32,
        )
        right_vals = displaced[right_rows]
        left_vals = displaced[left_rows]
        beyond = passed_along(left_vals, "sub", -1)
        multipliers = multipliers + DAMPING * (right_vals - beyond)
        if step + 1 < ITERS:
            previous = passed_along(multipliers, "sub", 1)
    return (displaced, multipliers)


def solution(mesh):
    placed = (
        P(("rve", "sub"), None),
        P(("rve", "sub"), None),
        P(("rve", "sub"), None),
        P("sub", None, None),
        P("sub", None),
        P("sub", None),
    )
    return jax.shard_map(
        local,
        mesh=mesh,
        in_specs=placed,
        out_specs=(P(("rve", "sub"), None), P(("rve", "sub"), None)),
        check_vma=False,
    )
```

profile of v0, /device:TPU:0, one launch (start us, length us, event | category | flops | bytes accessed | tf_op | source)
XLA Modules:
  0.0 172.6 jit_solution(9518307290389604258)
XLA Ops:
  0.6 1.1 copy.46
  4.0 1.5 scatter_custom_fusion
  5.5 1.6 scatter_custom_fusion.1
  7.1 10.4 %convolution_bitcast_fusion.2 = f32[1536,128]{0,1:T(8,128)S(1)} fusion(f32[1536,128]{1,0:T(8,128)S(1)} %scatter_custom_fusion.1, f32[1536,1536]{1,0:T(8,128)} %param.6), kind=kOutput, calls=%fused_computation.27 | convolution fusion | flops 3623878656 | bytes 11010048 | tf_op jit(solution)/shard_map/dot_general | solution.py:32
  17.8 1.1 scatter_custom_fusion.2
  18.9 25.5 %all_gather.9 = f32[1536,128]{1,0:T(8,128)S(1)} all-gather(f32[96,128]{1,0:T(8,128)S(1)} %scatter_custom_fusion.2), channel_id=1, replica_groups=mesh['rve'=2,'sub'=16] {'sub'}, dimensions={0}, use_global_device_ids=true | all-gather | bytes 835584 | tf_op jit(solution)/shard_map/all_gather | solution.py:37
  45.3 9.6 %copy.22 = f32[1536,1536]{0,1:T(8,128)} copy(f32[1536,1536]{1,0:T(8,128)} %param.6) | data formatting | bytes 18874368 | tf_op args[0]
  54.9 4.8 %gather_fusion = f32[96,1536]{1,0:T(8,128)S(1)} fusion(f32[1536,1536]{0,1:T(8,128)} %copy.22, s32[1024]{0:T(1024)S(1)} %pad_clamp_fusion.3), kind=kCustom, calls=%fused_computation | custom fusion | bytes 1180032 | tf_op jit(solution)/shard_map/gather | solution.py:26
  60.3 1.7 convolution_subtract_fusion.2
  62.0 1.4 copy.25
  64.8 1.2 collective-permute-done.1
  66.0 2.3 %collective-permute-start.2 = (f32[128,128]{1,0:T(8,128)S(1)}, f32[128,128]{1,0:T(8,128)S(1)}, u32[]{:S(2)}, u32[]{:S(2)}) collective-permute-start(f32[128,128]{1,0:T(8,128)S(1)} %subtract_multiply_fusion), channel_id=1, source_target_pairs={{0,1},{1,2},{2,3},{3,4},{4,5},{5,6},{6,7},{7,8},{8,9},{9,10},{10,1... | collective-permute-start | bytes 196616 | tf_op jit(solution)/shard_map/ppermute | solution.py:15
  68.4 1.5 scatter_custom_fusion.3
  69.9 2.6 %collective-permute-done.2 = f32[128,128]{1,0:T(8,128)S(1)} collective-permute-done((f32[128,128]{1,0:T(8,128)S(1)}, f32[128,128]{1,0:T(8,128)S(1)}, u32[]{:S(2)}, u32[]{:S(2)}) %collective-permute-start.2) | collective-permute-done | bytes 65568 | tf_op jit(solution)/shard_map/ppermute | solution.py:15
  72.5 1.7 scatter_fusion
  74.3 10.4 %convolution_bitcast_fusion.1 = f32[1536,128]{0,1:T(8,128)S(1)} fusion(f32[1536,128]{1,0:T(8,128)S(1)} %scatter_fusion, f32[1536,1536]{1,0:T(8,128)} %param.6), kind=kOutput, calls=%fused_computation.26 | convolution fusion | flops 3623878656 | bytes 11010048 | tf_op jit(solution)/shard_map/dot_general | solution.py:32
  85.0 1.1 scatter_custom_fusion.5
  86.1 19.7 %all_gather.10 = f32[1536,128]{1,0:T(8,128)S(1)} all-gather(f32[96,128]{1,0:T(8,128)S(1)} %scatter_custom_fusion.5), channel_id=1, replica_groups=mesh['rve'=2,'sub'=16] {'sub'}, dimensions={0}, use_global_device_ids=true | all-gather | bytes 835584 | tf_op jit(solution)/shard_map/all_gather | solution.py:37
  106.5 1.7 collective-permute-start.3
  108.2 1.5 collective-permute-done.3
  112.1 4.5 %collective-permute-start.4 = (f32[128,128]{1,0:T(8,128)S(1)}, f32[128,128]{1,0:T(8,128)S(1)}, u32[]{:S(2)}, u32[]{:S(2)}) collective-permute-start(f32[128,128]{1,0:T(8,128)S(1)} %gather_fusion.6), channel_id=1, source_target_pairs={{0,15},{1,0},{2,1},{3,2},{4,3},{5,4},{6,5},{7,6},{8,7},{9,8},{10,9... | collective-permute-start | bytes 196616 | tf_op jit(solution)/shard_map/ppermute | solution.py:15
  117.2 1.3 collective-permute-done.4
  118.6 1.6 scatter_custom_fusion.6
  120.1 4.9 %collective-permute-done.5 = f32[128,128]{1,0:T(8,128)S(1)} collective-permute-done((f32[128,128]{1,0:T(8,128)S(1)}, f32[128,128]{1,0:T(8,128)S(1)}, u32[]{:S(2)}, u32[]{:S(2)}) %collective-permute-start.5) | collective-permute-done | bytes 65568 | tf_op jit(solution)/shard_map/ppermute | solution.py:15
  125.0 1.8 %scatter_fusion.1 = f32[1536,128]{1,0:T(8,128)S(1)} fusion(f32[1536,128]{1,0:T(8,128)S(1)} %scatter_custom_fusion.6, s32[128]{0:T(128)S(1)} %get-tuple-element.12, f32[128,128]{1,0:T(8,128)S(1)} %collective-permute-done.5), kind=kCustom, calls=%fused_computation.20 | custom fusion | flops 16384 | bytes 197120 | tf_op jit(solution)/shard_map/scatter-add | solution.py:31
  126.8 10.4 %convolution_bitcast_fusion = f32[1536,128]{0,1:T(8,128)S(1)} fusion(f32[1536,128]{1,0:T(8,128)S(1)} %scatter_fusion.1, f32[1536,1536]{1,0:T(8,128)} %param.6), kind=kOutput, calls=%fused_computation.25 | convolution fusion | flops 3623878656 | bytes 11010048 | tf_op jit(solution)/shard_map/dot_general | solution.py:32
  137.5 1.1 scatter_custom_fusion.8
  138.6 19.6 %all_gather.11 = f32[1536,128]{1,0:T(8,128)S(1)} all-gather(f32[96,128]{1,0:T(8,128)S(1)} %scatter_custom_fusion.8), channel_id=1, replica_groups=mesh['rve'=2,'sub'=16] {'sub'}, dimensions={0}, use_global_device_ids=true | all-gather | bytes 835584 | tf_op jit(solution)/shard_map/all_gather | solution.py:37
  158.9 2.7 %collective-permute-start.6 = (f32[48,128]{1,0:T(8,128)S(1)}, f32[48,128]{1,0:T(8,128)S(1)}, u32[]{:S(2)}, u32[]{:S(2)}) collective-permute-start(f32[48,128]{1,0:T(8,128)S(1)} %convolution_add_fusion), channel_id=1, source_target_pairs={{0,15},{1,0},{2,1},{3,2},{4,3},{5,4},{6,5},{7,6},{8,7},{9,8},{10,9... | collective-permute-start | bytes 73736 | tf_op jit(solution)/shard_map/ppermute | solution.py:15
  161.6 1.5 collective-permute-done.6
  165.5 4.5 %collective-permute-start.7 = (f32[128,128]{1,0:T(8,128)S(1)}, f32[128,128]{1,0:T(8,128)S(1)}, u32[]{:S(2)}, u32[]{:S(2)}) collective-permute-start(f32[128,128]{1,0:T(8,128)S(1)} %gather_fusion.9), channel_id=1, source_target_pairs={{0,15},{1,0},{2,1},{3,2},{4,3},{5,4},{6,5},{7,6},{8,7},{9,8},{10,9... | collective-permute-start | bytes 196616 | tf_op jit(solution)/shard_map/ppermute | solution.py:15
  170.7 1.3 collective-permute-done.7
  (49 shorter events, 14.0 us)
Async XLA Ops:
  1.8 42.6 %copy-start = (f32[48,768]{1,0:T(8,128)S(1)}, f32[48,768]{1,0:T(8,128)}, u32[]{:S(2)}) copy-start(f32[48,768]{1,0:T(8,128)} %param.8) | copy-start | bytes 442372
  45.2 14.5 %collective-permute-start = (f32[48,128]{1,0:T(8,128)S(1)}, f32[48,128]{1,0:T(8,128)S(1)}, u32[]{:S(2)}, u32[]{:S(2)}) collective-permute-start(f32[48,128]{1,0:T(8,128)S(1)} %convolution_add_fusion.2), channel_id=1, source_target_pairs={{0,15},{1,0},{2,1},{3,2},{4,3},{5,4},{6,5},{7,6},{8,7},{9,8},{10,9... | collective-permute-start | bytes 73736 | tf_op jit(solution)/shard_map/ppermute | solution.py:15
  64.1 2.0 %collective-permute-start.1 = (f32[128,128]{1,0:T(8,128)S(1)}, f32[128,128]{1,0:T(8,128)S(1)}, u32[]{:S(2)}, u32[]{:S(2)}) collective-permute-start(f32[128,128]{1,0:T(8,128)S(1)} %gather_fusion.3), channel_id=1, source_target_pairs={{0,15},{1,0},{2,1},{3,2},{4,3},{5,4},{6,5},{7,6},{8,7},{9,8},{10,9... | collective-permute-start | bytes 196616 | tf_op jit(solution)/shard_map/ppermute | solution.py:15
  66.0 6.5 %collective-permute-start.2 = (f32[128,128]{1,0:T(8,128)S(1)}, f32[128,128]{1,0:T(8,128)S(1)}, u32[]{:S(2)}, u32[]{:S(2)}) collective-permute-start(f32[128,128]{1,0:T(8,128)S(1)} %subtract_multiply_fusion), channel_id=1, source_target_pairs={{0,1},{1,2},{2,3},{3,4},{4,5},{5,6},{6,7},{7,8},{8,9},{9,10},{10,1... | collective-permute-start | bytes 196616 | tf_op jit(solution)/shard_map/ppermute | solution.py:15
  106.5 3.2 %collective-permute-start.3 = (f32[48,128]{1,0:T(8,128)S(1)}, f32[48,128]{1,0:T(8,128)S(1)}, u32[]{:S(2)}, u32[]{:S(2)}) collective-permute-start(f32[48,128]{1,0:T(8,128)S(1)} %convolution_add_fusion.1), channel_id=1, source_target_pairs={{0,15},{1,0},{2,1},{3,2},{4,3},{5,4},{6,5},{7,6},{8,7},{9,8},{10,9... | collective-permute-start | bytes 73736 | tf_op jit(solution)/shard_map/ppermute | solution.py:15
  112.1 6.4 %collective-permute-start.4 = (f32[128,128]{1,0:T(8,128)S(1)}, f32[128,128]{1,0:T(8,128)S(1)}, u32[]{:S(2)}, u32[]{:S(2)}) collective-permute-start(f32[128,128]{1,0:T(8,128)S(1)} %gather_fusion.6), channel_id=1, source_target_pairs={{0,15},{1,0},{2,1},{3,2},{4,3},{5,4},{6,5},{7,6},{8,7},{9,8},{10,9... | collective-permute-start | bytes 196616 | tf_op jit(solution)/shard_map/ppermute | solution.py:15
  118.5 6.5 %collective-permute-start.5 = (f32[128,128]{1,0:T(8,128)S(1)}, f32[128,128]{1,0:T(8,128)S(1)}, u32[]{:S(2)}, u32[]{:S(2)}) collective-permute-start(f32[128,128]{1,0:T(8,128)S(1)} %multiply_add_fusion.1), channel_id=1, source_target_pairs={{0,1},{1,2},{2,3},{3,4},{4,5},{5,6},{6,7},{7,8},{8,9},{9,10},{10,1... | collective-permute-start | bytes 196616 | tf_op jit(solution)/shard_map/ppermute | solution.py:15
  158.9 4.2 %collective-permute-start.6 = (f32[48,128]{1,0:T(8,128)S(1)}, f32[48,128]{1,0:T(8,128)S(1)}, u32[]{:S(2)}, u32[]{:S(2)}) collective-permute-start(f32[48,128]{1,0:T(8,128)S(1)} %convolution_add_fusion), channel_id=1, source_target_pairs={{0,15},{1,0},{2,1},{3,2},{4,3},{5,4},{6,5},{7,6},{8,7},{9,8},{10,9... | collective-permute-start | bytes 73736 | tf_op jit(solution)/shard_map/ppermute | solution.py:15
  164.9 7.7 %copy-start.1 = (f32[1536,128]{1,0:T(8,128)}, f32[1536,128]{1,0:T(8,128)S(1)}, u32[]{:S(2)}) copy-start(f32[1536,128]{1,0:T(8,128)S(1)} %copy.35) | copy-start | bytes 2359300
  165.5 6.4 %collective-permute-start.7 = (f32[128,128]{1,0:T(8,128)S(1)}, f32[128,128]{1,0:T(8,128)S(1)}, u32[]{:S(2)}, u32[]{:S(2)}) collective-permute-start(f32[128,128]{1,0:T(8,128)S(1)} %gather_fusion.9), channel_id=1, source_target_pairs={{0,15},{1,0},{2,1},{3,2},{4,3},{5,4},{6,5},{7,6},{8,7},{9,8},{10,9... | collective-permute-start | bytes 196616 | tf_op jit(solution)/shard_map/ppermute | solution.py:15
where the time goes:
time: 173 us
  blocking collectives  64.8 us (37%)
  matrix products  36.7 us (21%)
  local copies, waits for them, and re-layouts  27.5 us (16%)
  starting transfers between devices  15.8 us (9%)
  waiting for transfers between devices  14.3 us (8%)
  other arithmetic  12.5 us (7%)
    all_gather x3, blocking collectives, local(): piece = lax.all_gather(slotted, 'sub', axis=0, tiled=True)  64.8 us
    dot_general x3, matrix products, local(): jnp.dot(condensed, loads, precision=lax.Precision.HIGHEST, preferred_elem...  31.3 us
    ppermute x8, starting transfers between devices, passed_along(): return lax.ppermute(value, axis, pairs)  15.8 us
    ppermute x8, waiting for transfers between devices, passed_along(): return lax.ppermute(value, axis, pairs)  14.3 us
    unnamed x9, local copies, waits for them, and re-layouts  11.1 us
    scatter-add x6, other arithmetic, local(): eigen_loads.at[right_rows].add(-multipliers).at[left_rows].add(previous)  9.69 us
    gather x1, local copies, waits for them, and re-layouts, local(): prolong = condensed[:, prim_rows]  4.76 us
  transfers between devices with their start and end apart: 8, of which 7 were waited for; matrix products, arithmetic and copies ran while one was open for 11% of the time, Pallas kernels for 0%

commit v1 on v0

v1 whole, which is shorter than its diff:
```python
import functools

import jax
import jax.numpy as jnp
from jax import lax
from jax.experimental import pallas as pl
from jax.experimental.pallas import tpu as pltpu
from jax.sharding import PartitionSpec as P

ITERS = 3
DAMPING = 0.5
MESH = pl.DeviceIdType.MESH
F32 = jnp.float32
BF16 = jnp.bfloat16
LANES = 128


def grid_of(count):
    chips = count // 2
    inner = 1
    while (2 * inner) ** 2 <= chips and chips % (2 * inner) == 0:
        inner *= 2
    return chips // inner, inner


def flipped(index, mask, count):
    if count & (count - 1):
        return lax.rem(index + count - mask, count)
    out = 0
    bit = 1
    while bit < count:
        own = lax.rem(index // bit, 2)
        out = out + bit * ((1 - own) if mask & bit else own)
        bit *= 2
    return out


def returned(index, mask, count):
    if count & (count - 1):
        return lax.rem(index + mask, count)
    return flipped(index, mask, count)


def split(value):
    high = value.astype(BF16)
    return high, (value - high.astype(F32)).astype(BF16)


def product(high, low, value):
    value_high, value_low = split(value)
    return product_parts(high, low, value_high, value_low)


def product_parts(high, low, value_high, value_low):
    width = value_high.shape[1]
    both = jnp.dot(high, jnp.concatenate([value_high, value_low], axis=1), preferred_element_type=F32)
    return both[:, :width] + both[:, width:] + jnp.dot(low, value_high, preferred_element_type=F32)


def kernel(
    count, primal, width, ids_s, ids_v, k_hbm, f_ref, cinv_ref, u_ref, lam_ref,
    k_ref, kh_ref, kl_ref, e_ref, fh_ref, fl_ref, ks_ref, ah_ref, al_ref, cols_ref, ch_ref, cl_ref,
    kph_ref, kpl_ref, pre_ref, gat_ref, r_ref, send_r, send_l, got_r, got_l, send_ar, send_al, got_ar, got_al,
    k_sem, send_sem, block_sem, face_sem, cinv_send, cinv_recv, a_send, a_recv,
):
    outer, inner = grid_of(count)
    order, columns = f_ref.shape
    owned = primal // 2
    tile = order // k_sem.shape[0]
    padded = e_ref.shape[1]
    me = lax.axis_index("sub")
    core = lax.rem(me, 2)
    y = lax.rem(me // 2, inner)
    z = me // (2 * inner)

    def at(z_, y_, core_):
        return (z_ * inner + y_) * 2 + core_

    def around(steps):
        return lax.rem(me + (steps + count), count)

    def k_copy(c):
        rows = pl.ds(c * tile, tile)
        return pltpu.make_async_copy(k_hbm.at[rows, :], k_ref.at[rows, :], k_sem.at[c])

    for c in range(k_sem.shape[0]):
        k_copy(c).start()

    outer_peers = [at(flipped(z, m, outer), y, core) for m in range(1, outer)]
    outer_back = [returned(z, m, outer) for m in range(1, outer)]
    inner_peers = [at(z, flipped(y, m, inner), core) for m in range(1, inner)]
    partner = at(z, y, 1 - core)
    ring = [around(d) for d in (-2, -1, 1, 2)]

    barrier = pltpu.get_barrier_semaphore()
    greeted = outer_peers + inner_peers + [partner] + ring
    if outer & (outer - 1):
        greeted = greeted + [at(b, y, core) for b in outer_back]
    for peer in greeted:
        pl.semaphore_signal(barrier, inc=1, device_id={"sub": peer}, device_id_type=MESH)
    pl.semaphore_wait(barrier, len(greeted))

    def remote(src, dst, ssem, rsem, peer):
        return pltpu.make_async_remote_copy(
            src_ref=src, dst_ref=dst, send_sem=ssem, recv_sem=rsem, device_id={"sub": peer}, device_id_type=MESH
        )

    cinv_copies = [
        remote(cinv_ref, cols_ref.at[slot], cinv_send.at[slot], cinv_recv.at[slot], around(d))
        for slot, d in ((0, 1), (1, -1), (2, -2))
    ]
    for copy in cinv_copies:
        copy.start()

    for c in range(order // tile):
        rows = lax.broadcasted_iota(jnp.int32, (tile, padded), 0) + c * tile
        e_ref[c * tile:(c + 1) * tile, :] = jnp.where(rows == ids_v[...], 1.0, 0.0).astype(BF16)
    fh, fl = split(f_ref[...])
    fh_ref[...] = fh
    fl_ref[...] = fl

    for c in range(k_sem.shape[0]):
        k_copy(c).wait()

    used = 2 * width + primal
    if padded > used:
        ks_ref[used:, :] = jnp.zeros((padded - used, order), F32)

    @pl.loop(0, used // 8)
    def _(i):
        base = pl.multiple_of(i * 8, 8)
        for j in range(8):
            ks_ref[pl.ds(base + j, 1), :] = k_ref[pl.ds(ids_s[0, base + j], 1), :]

    ksh, ksl = split(ks_ref[...])
    first = product_parts(ksh, ksl, fh_ref[...], fl_ref[...])

    def finish_a():
        high, low = split(ks_ref[...])
        a_high = jnp.dot(high, e_ref[...], preferred_element_type=F32)
        a_low = jnp.dot(low, e_ref[...], preferred_element_type=F32)
        ah_ref[...] = a_high.astype(BF16)
        al_ref[...] = a_low.astype(BF16)
        corner = (a_high + a_low)[:2 * width, 2 * width:]
        send_ar[...] = corner[:width]
        send_al[...] = corner[width:]

    def split_k():
        @pl.loop(0, order // tile)
        def _(c):
            rows = pl.ds(pl.multiple_of(c * tile, tile), tile)
            high, low = split(k_ref[rows, :])
            kh_ref[rows, :] = high
            kl_ref[rows, :] = low

    def primal_columns():
        picks = e_ref[:, 2 * width:]

        @pl.loop(0, order // tile)
        def _(c):
            rows = pl.ds(pl.multiple_of(c * tile, tile), tile)
            kph_ref[rows, :] = jnp.dot(kh_ref[rows, :], picks, preferred_element_type=F32).astype(BF16)
            kpl_ref[rows, :] = jnp.dot(kl_ref[rows, :], picks, preferred_element_type=F32).astype(BF16)

    def uncorrected(changes):
        high, low = split(changes)
        spread = jnp.dot(e_ref[:, :2 * width], jnp.concatenate([high, low], axis=1), preferred_element_type=F32)
        loads = f_ref[...] + (spread[:, :columns] + spread[:, columns:])
        high, low = split(loads)
        fh_ref[...] = high
        fl_ref[...] = low

        @pl.loop(0, order // tile)
        def _(c):
            rows = pl.ds(pl.multiple_of(c * tile, tile), tile)
            pre_ref[rows, :] = product_parts(kh_ref[rows, :], kl_ref[rows, :], fh_ref[...], fl_ref[...])

    a_copies = [
        remote(send_al, got_al, a_send.at[0], a_recv.at[0], around(-1)),
        remote(send_ar, got_ar, a_send.at[1], a_recv.at[1], around(1)),
    ]

    lam = jnp.zeros((width, columns), F32)
    lam_before = jnp.zeros((width, columns), F32)
    values = first
    changes = None
    for step in range(ITERS):
        if step:
            changes = jnp.concatenate([-lam, lam_before], axis=0)
            values = first + product(ah_ref[:, :2 * width], al_ref[:, :2 * width], changes)
        gat = gat_ref.at[step]
        gat_ref[step, me] = values[2 * width:2 * width + primal]
        send_r[step] = values[:width]
        send_l[step] = values[width:2 * width]
        started = []

        def forward(block, peer):
            copy = remote(
                gat.at[block], gat.at[block], send_sem.at[step, len(started)], block_sem.at[step, block], peer
            )
            copy.start()
            started.append(copy)

        def arrived(block):
            remote(gat.at[block], gat.at[block], send_sem.at[step, 0], block_sem.at[step, block], partner).wait_recv()

        for peer in reversed(outer_peers):
            forward(me, peer)
        for peer in inner_peers:
            forward(me, peer)
        forward(me, partner)
        faces = [
            remote(send_l.at[step], got_l.at[step], face_sem.at[0, step, 0], face_sem.at[1, step, 0], around(-1)),
            remote(send_r.at[step], got_r.at[step], face_sem.at[0, step, 1], face_sem.at[1, step, 1], around(1)),
        ]
        for copy in faces:
            copy.start()

        if step == 0:
            finish_a()
            for copy in a_copies:
                copy.start()
        if step == 1:
            primal_columns()
        if step == ITERS - 1:
            uncorrected(changes)

        for source in outer_back:
            block = at(source, y, core)
            arrived(block)
            for peer in inner_peers:
                forward(block, peer)
            forward(block, partner)
        if step == 0:
            split_k()
            for copy in cinv_copies:
                copy.wait()
            for slot, part in enumerate((cols_ref.at[0], cinv_ref, cols_ref.at[1], cols_ref.at[2])):
                high, low = split(part[...])
                ch_ref[slot * owned:(slot + 1) * owned, :] = high
                cl_ref[slot * owned:(slot + 1) * owned, :] = low
        for m in range(1, inner):
            for source in [z] + outer_back:
                block = at(source, returned(y, m, inner), core)
                arrived(block)
                forward(block, partner)
        for source in [z] + outer_back:
            for m in range(inner):
                arrived(at(source, y if m == 0 else returned(y, m, inner), 1 - core))

        for s in range(count):
            r_ref[s * owned:(s + 1) * owned, :] = (
                gat_ref[step, s, :owned, :] + gat_ref[step, (s - 1) % count, owned:, :]
            )
        coarse = product(ch_ref[...], cl_ref[...], r_ref[...])
        fill = jnp.zeros((padded - 2 * width - primal, columns), F32)

        def steps_of(slot):
            return jnp.concatenate([coarse[slot * owned:(slot + 2) * owned], fill], axis=0)

        q_before, q_own, q_after = steps_of(0), steps_of(1), steps_of(2)
        own = product(ah_ref[:2 * width, 2 * width:], al_ref[:2 * width, 2 * width:], q_own)
        if step == 0:
            for copy in a_copies:
                copy.wait()
        for copy in faces:
            copy.wait()
        after = product(*split(got_al[...]), q_after)
        lam = lam + DAMPING * ((values[:width] - own[:width]) - (got_l[step] - after))
        if step + 1 < ITERS:
            before = product(*split(got_ar[...]), q_before)
            lam_before = lam_before + DAMPING * ((got_r[step] - before) - (values[width:2 * width] - own[width:]))
        else:
            lam_ref[...] = lam
            q_high, q_low = split(q_own)

            @pl.loop(0, order // tile)
            def _(c):
                rows = pl.ds(pl.multiple_of(c * tile, tile), tile)
                u_ref[rows, :] = pre_ref[rows, :] - product_parts(kph_ref[rows, :], kpl_ref[rows, :], q_high, q_low)
        for copy in started:
            copy.wait_send()


def local(condensed, eigen_loads, coarse_inverse, face_rows, primal_rows, primal_slot):
    count = lax.axis_size("sub")
    order, columns = eigen_loads.shape
    owned, total = coarse_inverse.shape
    width = face_rows.shape[2]
    primal = primal_rows.shape[1]
    padded = 2 * width + -(-primal // LANES) * LANES
    outer, inner = grid_of(count)
    slots = lax.broadcasted_iota(jnp.int32, (primal, primal), 0)
    ordered = jnp.sum(jnp.where(primal_slot == slots, primal_rows, 0), axis=1)
    fill = jnp.full((padded - 2 * width - primal,), -1, jnp.int32)
    ids = jnp.concatenate([face_rows[0, 1], face_rows[0, 0], ordered, fill])[None]
    tile = 256 if order % 256 == 0 else order
    sends = (outer - 1) + (inner - 1) * outer + outer * inner
    dma = pltpu.SemaphoreType.DMA
    vmem = pl.BlockSpec(memory_space=pltpu.VMEM)
    face = pltpu.VMEM((ITERS, width, columns), F32)
    corner = pltpu.VMEM((width, padded - 2 * width), F32)
    return pl.pallas_call(
        functools.partial(kernel, count, primal, width),
        out_shape=(
            jax.ShapeDtypeStruct((order, columns), F32),
            jax.ShapeDtypeStruct((width, columns), F32),
        ),
        in_specs=[pl.BlockSpec(memory_space=pltpu.SMEM), vmem, pl.BlockSpec(memory_space=pl.ANY), vmem, vmem],
        out_specs=(vmem, vmem),
        scratch_shapes=[
            pltpu.VMEM((order, order), F32),
            pltpu.VMEM((order, order), BF16),
            pltpu.VMEM((order, order), BF16),
            pltpu.VMEM((order, padded), BF16),
            pltpu.VMEM((order, columns), BF16),
            pltpu.VMEM((order, columns), BF16),
            pltpu.VMEM((padded, order), F32),
            pltpu.VMEM((padded, padded), BF16),
            pltpu.VMEM((padded, padded), BF16),
            pltpu.VMEM((3, owned, total), F32),
            pltpu.VMEM((4 * owned, total), BF16),
            pltpu.VMEM((4 * owned, total), BF16),
            pltpu.VMEM((order, padded - 2 * width), BF16),
            pltpu.VMEM((order, padded - 2 * width), BF16),
            pltpu.VMEM((order, columns), F32),
            pltpu.VMEM((ITERS, count, primal, columns), F32),
            pltpu.VMEM((total, columns), F32),
            face, face, face, face,
            corner, corner, corner, corner,
            dma((order // tile,)),
            dma((ITERS, sends)),
            dma((ITERS, count)),
            dma((2, ITERS, 2)),
            dma((3,)),
            dma((3,)),
            dma((2,)),
            dma((2,)),
        ],
        compiler_params=pltpu.CompilerParams(
            collective_id=0, has_side_effects=True, vmem_limit_bytes=67043328
        ),
    )(ids, ids, condensed, eigen_loads, coarse_inverse)


def solution(mesh):
    placed = (
        P(("rve", "sub"), None),
        P(("rve", "sub"), None),
        P(("rve", "sub"), None),
        P("sub", None, None),
        P("sub", None),
        P("sub", None),
    )
    return jax.shard_map(
        local,
        mesh=mesh,
        in_specs=placed,
        out_specs=(P(("rve", "sub"), None), P(("rve", "sub"), None)),
        check_vma=False,
    )
```

time: 173 us -> 57.9 us (0.33)
  blocking collectives: 64.8 us -> 0 us
  Pallas kernels: 0 us -> 51.3 us
  matrix products: 36.7 us -> 0 us
  local copies, waits for them, and re-layouts: 27.5 us -> 4.87 us
  starting transfers between devices: 15.8 us -> 0 us
  waiting for transfers between devices: 14.3 us -> 0 us
  other arithmetic: 12.5 us -> 0.86 us
    all_gather x3 -> x0, blocking collectives: 64.8 us -> none  [local(): piece = lax.all_gather(slotted, 'sub', axis=0, tiled=True)]
    pallas_call x0 -> x1, Pallas kernels: none -> 51.3 us  [local(): pl.pallas_call(functools.partial(kernel, count, primal, width), out_shape...]
    dot_general x12 -> x0, matrix products: 36.7 us -> none  [the longest x3 31.3 us: local(): jnp.dot(condensed, loads, precision=lax.Precision.HIGHEST, preferred_elem...]
    ppermute x8 -> x0, starting transfers between devices: 15.8 us -> none  [passed_along(): return lax.ppermute(value, axis, pairs)]
    ppermute x8 -> x0, waiting for transfers between devices: 14.3 us -> none  [passed_along(): return lax.ppermute(value, axis, pairs)]
    gather x10 -> x0, local copies, waits for them, and re-layouts: 10.5 us -> none  [the longest x1 4.76 us: local(): prolong = condensed[:, prim_rows]]
    scatter-add x6 -> x0, other arithmetic: 9.69 us -> none  [local(): eigen_loads.at[right_rows].add(-multipliers).at[left_rows].add(previous)]
    unnamed x9 -> x2, local copies, waits for them, and re-layouts: 11.1 us -> 3.54 us
  transfers between devices with their start and end apart: 8 -> 0, of which waited for: 7 -> 0; matrix products, arithmetic and copies ran while one was open for 11% -> 0% of each run, Pallas kernels for 0% -> 0%
where the time goes in v1:
time: 57.9 us; the launch traced here: 57.7 us
  Pallas kernels  51.3 us (89%)
  local copies, waits for them, and re-layouts  4.87 us (8%)
  other arithmetic  0.86 us (1%)
  between operations  0.65 us (1%)
    pallas_call x1, Pallas kernels, local(): pl.pallas_call(functools.partial(kernel, count, primal, width), out_shape...  51.3 us
    unnamed x2, local copies, waits for them, and re-layouts  3.54 us

profile of v1, /device:TPU:0, one launch (start us, length us, event | category | flops | bytes accessed | tf_op | source)
XLA Modules:
  0.0 57.7 jit_solution(16165101003741641403)
XLA Ops:
  0.6 0.8 %select_reduce_fusion = s32[96]{0:T(128)S(1)} fusion(s32[96]{0:T(128)} %bitcast.6, s32[96]{0:T(128)} %bitcast.7), kind=kLoop, calls=%fused_computation | loop fusion | flops 27552 | bytes 1152 | tf_op jit(solution)/shard_map/reduce_sum | solution.py:294
  1.4 0.8 %slice_bitcast_fusion.1 = (s32[128]{0:T(128)S(1)}, s32[128]{0:T(128)S(1)}) fusion(s32[1,2,128]{2,1,0:T(2,128)} %param.9), kind=kLoop, calls=%fused_computation.4 | loop fusion | bytes 2048 | tf_op jit(solution)/shard_map/squeeze | solution.py:296
  2.2 0.1 pad_add_fusion
  2.3 0.6 broadcast_in_dim.24.ids_s.ids_v
  2.8 51.3 %shard_map.77 = (f32[1536,128]{1,0:T(8,128)}, f32[128,128]{1,0:T(8,128)}) custom-call(s32[1,384]{1,0:T(1,128)} %broadcast_in_dim.24.ids_s.ids_v, s32[1,384]{1,0:T(1,128)} %broadcast_in_dim.24.ids_s.ids_v, f32[1536,1536]{1,0:T(8,128)} %k_hbm.1, f32[1536,128]{1,0:T(8,128)} %f_ref.1, f32[48,768]{1,0:T(8,128)} %cinv_ref.1), custom_call_target="tpu_custom_call" | custom-call | tf_op jit(solution)/shard_map/pallas_call | solution.py:303
  54.2 2.1 %copy.10 = f32[1536,128]{1,0:T(8,128)} copy(f32[1536,128]{1,0:T(8,128)} %get-tuple-element.6) | data formatting | bytes 1572864
  56.2 1.5 %copy.11 = f32[128,128]{1,0:T(8,128)} copy(f32[128,128]{1,0:T(8,128)} %get-tuple-element.7) | data formatting | bytes 131072
  (1 shorter events, 0.0 us)

commit v2 on v1

--- a/solution.py
+++ b/solution.py
@@ -9,6 +9,7 @@
 
 ITERS = 3
 DAMPING = 0.5
+VMEM_LIMIT = 67043328
 MESH = pl.DeviceIdType.MESH
 F32 = jnp.float32
 BF16 = jnp.bfloat16
@@ -58,9 +59,9 @@
 
 
 def kernel(
-    count, primal, width, ids_s, ids_v, k_hbm, f_ref, cinv_ref, u_ref, lam_ref,
-    k_ref, kh_ref, kl_ref, e_ref, fh_ref, fl_ref, ks_ref, ah_ref, al_ref, cols_ref, ch_ref, cl_ref,
-    kph_ref, kpl_ref, pre_ref, gat_ref, r_ref, send_r, send_l, got_r, got_l, send_ar, send_al, got_ar, got_al,
+    count, primal, width, face_s, prim_s, face_hbm, prim_hbm, slot_hbm, k_hbm, f_hbm, cinv_hbm, pre_ref, kph_ref, kpl_ref, q_ref, lam_ref,
+    face_v, prim_v, slot_v, f_ref, cinv_ref, in_sem, k_ref, kh_ref, kl_ref, e_ref, fh_ref, fl_ref, ks_ref, first_ref, ah_ref, al_ref, cols_ref, ch_ref, cl_ref,
+    gat_ref, r_ref, send_r, send_l, got_r, got_l, send_ar, send_al, got_ar, got_al,
     k_sem, send_sem, block_sem, face_sem, cinv_send, cinv_recv, a_send, a_recv,
 ):
     outer, inner = grid_of(count)
@@ -83,6 +84,14 @@
         rows = pl.ds(c * tile, tile)
         return pltpu.make_async_copy(k_hbm.at[rows, :], k_ref.at[rows, :], k_sem.at[c])
 
+    held = [
+        pltpu.make_async_copy(src, dst, in_sem.at[i])
+        for i, (src, dst) in enumerate((
+            (f_hbm, f_ref), (cinv_hbm, cinv_ref), (face_hbm, face_v), (prim_hbm, prim_v), (slot_hbm, slot_v)
+        ))
+    ]
+    for copy in held:
+        copy.start()
     for c in range(k_sem.shape[0]):
         k_copy(c).start()
 
@@ -90,7 +99,7 @@
     outer_back = [returned(z, m, outer) for m in range(1, outer)]
     inner_peers = [at(z, flipped(y, m, inner), core) for m in range(1, inner)]
     partner = at(z, y, 1 - core)
-    ring = [around(d) for d in (-2, -1, 1, 2)]
+    ring = [around(d) for d in (-1, 1)]
 
     barrier = pltpu.get_barrier_semaphore()
     greeted = outer_peers + inner_peers + [partner] + ring
@@ -98,7 +107,6 @@
         greeted = greeted + [at(b, y, core) for b in outer_back]
     for peer in greeted:
         pl.semaphore_signal(barrier, inc=1, device_id={"sub": peer}, device_id_type=MESH)
-    pl.semaphore_wait(barrier, len(greeted))
 
     def remote(src, dst, ssem, rsem, peer):
         return pltpu.make_async_remote_copy(
@@ -107,51 +115,99 @@
 
     cinv_copies = [
         remote(cinv_ref, cols_ref.at[slot], cinv_send.at[slot], cinv_recv.at[slot], around(d))
-        for slot, d in ((0, 1), (1, -1), (2, -2))
+        for slot, d in ((0, 1), (1, -1))
     ]
-    for copy in cinv_copies:
-        copy.start()
-
-    for c in range(order // tile):
-        rows = lax.broadcasted_iota(jnp.int32, (tile, padded), 0) + c * tile
-        e_ref[c * tile:(c + 1) * tile, :] = jnp.where(rows == ids_v[...], 1.0, 0.0).astype(BF16)
+    passed_on = remote(cols_ref.at[1], cols_ref.at[2], cinv_send.at[2], cinv_recv.at[2], around(-1))
+
+    for copy in held:
+        copy.wait()
+
+    square = (primal, primal)
+    eye = lax.broadcasted_iota(jnp.int32, square, 0) == lax.broadcasted_iota(jnp.int32, square, 1)
+    prim_col = jnp.sum(jnp.where(eye, prim_v[...].astype(F32), 0.0), axis=1, keepdims=True)
+    slot_col = jnp.sum(jnp.where(eye, slot_v[...].astype(F32), 0.0), axis=1, keepdims=True)
+    corner_width = padded - 2 * width
+    lane = lax.broadcasted_iota(jnp.int32, (primal, corner_width), 1).astype(F32)
+    ordered = jnp.sum(jnp.where(slot_col == lane, prim_col + 1.0, 0.0), axis=0, keepdims=True) - 1.0
+    ordering = jnp.where(lax.broadcasted_iota(jnp.int32, square, 0) == slot_v[...], 1.0, 0.0).astype(BF16)
+
     fh, fl = split(f_ref[...])
     fh_ref[...] = fh
     fl_ref[...] = fl
 
-    for c in range(k_sem.shape[0]):
-        k_copy(c).wait()
-
-    used = 2 * width + primal
-    if padded > used:
-        ks_ref[used:, :] = jnp.zeros((padded - used, order), F32)
-
-    @pl.loop(0, used // 8)
-    def _(i):
-        base = pl.multiple_of(i * 8, 8)
-        for j in range(8):
-            ks_ref[pl.ds(base + j, 1), :] = k_ref[pl.ds(ids_s[0, base + j], 1), :]
-
-    ksh, ksl = split(ks_ref[...])
-    first = product_parts(ksh, ksl, fh_ref[...], fl_ref[...])
-
-    def finish_a():
-        high, low = split(ks_ref[...])
-        a_high = jnp.dot(high, e_ref[...], preferred_element_type=F32)
-        a_low = jnp.dot(low, e_ref[...], preferred_element_type=F32)
-        ah_ref[...] = a_high.astype(BF16)
-        al_ref[...] = a_low.astype(BF16)
-        corner = (a_high + a_low)[:2 * width, 2 * width:]
-        send_ar[...] = corner[:width]
-        send_al[...] = corner[width:]
-
-    def split_k():
-        @pl.loop(0, order // tile)
+    def stream(first_tile, last_tile):
+        @pl.loop(first_tile, last_tile)
         def _(c):
+            k_copy(c).wait()
             rows = pl.ds(pl.multiple_of(c * tile, tile), tile)
             high, low = split(k_ref[rows, :])
             kh_ref[rows, :] = high
             kl_ref[rows, :] = low
+            pre_ref[rows, :] = product_parts(high, low, fh_ref[...], fl_ref[...])
+
+    half = 1
+    stream(0, half)
+    pl.semaphore_wait(barrier, len(greeted))
+    for copy in cinv_copies:
+        copy.start()
+    stream(half, order // tile)
+
+    used = 2 * width + primal
+
+    def picked(to_ref, from_ref):
+        def rows_of(start, size, row_at):
+            @pl.loop(0, size // 8)
+            def _(i):
+                base = pl.multiple_of(i * 8, 8)
+                for j in range(8):
+                    to_ref[pl.ds(start + base + j, 1), :] = from_ref[pl.ds(row_at(base + j), 1), :]
+
+        rows_of(0, width, lambda i: face_s[0, 1, i])
+        rows_of(width, width, lambda i: face_s[0, 0, i])
+        rows_of(2 * width, primal, lambda i: prim_s[0, i])
+
+    def in_order(value):
+        high, low = split(value)
+        half_width = value.shape[1]
+        both = jnp.dot(ordering, jnp.concatenate([high, low], axis=1), preferred_element_type=F32)
+        return both[:, :half_width] + both[:, half_width:]
+
+    picked(first_ref, pre_ref)
+    empty = jnp.zeros((padded - used, columns), F32)
+    first = jnp.concatenate([first_ref[:2 * width], in_order(first_ref[2 * width:used]), empty], axis=0)
+
+    def one_hot_columns():
+        right_ids, left_ids = face_v[0, 1:2, :], face_v[0, 0:1, :]
+        ordered_ids = ordered.astype(jnp.int32)
+
+        @pl.loop(0, order // tile)
+        def _(c):
+            rows = pl.ds(pl.multiple_of(c * tile, tile), tile)
+            near = lax.broadcasted_iota(jnp.int32, (tile, width), 0) + c * tile
+            e_ref[rows, :width] = jnp.where(near == right_ids, 1.0, 0.0).astype(BF16)
+            e_ref[rows, width:2 * width] = jnp.where(near == left_ids, 1.0, 0.0).astype(BF16)
+            near = lax.broadcasted_iota(jnp.int32, (tile, corner_width), 0) + c * tile
+            e_ref[rows, 2 * width:] = jnp.where(near == ordered_ids, 1.0, 0.0).astype(BF16)
+
+    def finish_a():
+        one_hot_columns()
+        if padded > used:
+            ks_ref[used:, :] = jnp.zeros((padded - used, order), F32)
+        picked(ks_ref, k_ref)
+        high, low = split(ks_ref[...])
+        parts = []
+        for part, out in ((high, ah_ref), (low, al_ref)):
+            found = jnp.dot(part, e_ref[...], preferred_element_type=F32)
+            out[:2 * width, :] = found[:2 * width].astype(BF16)
+            out[2 * width:used, :] = jnp.dot(
+                ordering, found[2 * width:used].astype(BF16), preferred_element_type=F32
+            ).astype(BF16)
+            if padded > used:
+                out[used:, :] = jnp.zeros((padded - used, padded), BF16)
+            parts.append(found[:2 * width, 2 * width:])
+        corner = parts[0] + parts[1]
+        send_ar[...] = corner[:width]
+        send_al[...] = corner[width:]
 
     def primal_columns():
         picks = e_ref[:, 2 * width:]
@@ -194,21 +250,22 @@
         send_l[step] = values[width:2 * width]
         started = []
 
-        def forward(block, peer):
-            copy = remote(
-                gat.at[block], gat.at[block], send_sem.at[step, len(started)], block_sem.at[step, block], peer
-            )
+        def forward(block, peer, part):
+            rows = gat.at[block, pl.ds(part * owned, owned)]
+            copy = remote(rows, rows, send_sem.at[step, len(started)], block_sem.at[step, block, part], peer)
             copy.start()
             started.append(copy)
 
-        def arrived(block):
-            remote(gat.at[block], gat.at[block], send_sem.at[step, 0], block_sem.at[step, block], partner).wait_recv()
-
-        for peer in reversed(outer_peers):
-            forward(me, peer)
-        for peer in inner_peers:
-            forward(me, peer)
-        forward(me, partner)
+        def arrived(block, part):
+            rows = gat.at[block, pl.ds(part * owned, owned)]
+            remote(rows, rows, send_sem.at[step, 0], block_sem.at[step, block, part], partner).wait_recv()
+
+        for part in range(2):
+            for peer in reversed(outer_peers):
+                forward(me, peer, part)
+            for peer in inner_peers:
+                forward(me, peer, part)
+            forward(me, partner, part)
         faces = [
             remote(send_l.at[step], got_l.at[step], face_sem.at[0, step, 0], face_sem.at[1, step, 0], around(-1)),
             remote(send_r.at[step], got_r.at[step], face_sem.at[0, step, 1], face_sem.at[1, step, 1], around(1)),
@@ -217,6 +274,8 @@
             copy.start()
 
         if step == 0:
+            cinv_copies[1].wait_recv()
+            passed_on.start()
             finish_a()
             for copy in a_copies:
                 copy.start()
@@ -225,28 +284,31 @@
         if step == ITERS - 1:
             uncorrected(changes)
 
-        for source in outer_back:
-            block = at(source, y, core)
-            arrived(block)
-            for peer in inner_peers:
-                forward(block, peer)
-            forward(block, partner)
+        for part in range(2):
+            for source in outer_back:
+                block = at(source, y, core)
+                arrived(block, part)
+                for peer in inner_peers:
+                    forward(block, peer, part)
+                forward(block, partner, part)
         if step == 0:
-            split_k()
-            for copy in cinv_copies:
-                copy.wait()
+            cinv_copies[0].wait()
+            cinv_copies[1].wait_send()
+            passed_on.wait()
             for slot, part in enumerate((cols_ref.at[0], cinv_ref, cols_ref.at[1], cols_ref.at[2])):
                 high, low = split(part[...])
                 ch_ref[slot * owned:(slot + 1) * owned, :] = high
                 cl_ref[slot * owned:(slot + 1) * owned, :] = low
-        for m in range(1, inner):
+        for part in range(2):
+            for m in range(1, inner):
+                for source in [z] + outer_back:
+                    block = at(source, returned(y, m, inner), core)
+                    arrived(block, part)
+                    forward(block, partner, part)
+        for part in range(2):
             for source in [z] + outer_back:
-                block = at(source, returned(y, m, inner), core)
-                arrived(block)
-                forward(block, partner)
-        for source in [z] + outer_back:
-            for m in range(inner):
-                arrived(at(source, y if m == 0 else returned(y, m, inner), 1 - core))
+                for m in range(inner):
+                    arrived(at(source, y if m == 0 else returned(y, m, inner), 1 - core), part)
 
         for s in range(count):
             r_ref[s * owned:(s + 1) * owned, :] = (
@@ -272,14 +334,14 @@
             lam_before = lam_before + DAMPING * ((got_r[step] - before) - (values[width:2 * width] - own[width:]))
         else:
             lam_ref[...] = lam
-            q_high, q_low = split(q_own)
-
-            @pl.loop(0, order // tile)
-            def _(c):
-                rows = pl.ds(pl.multiple_of(c * tile, tile), tile)
-                u_ref[rows, :] = pre_ref[rows, :] - product_parts(kph_ref[rows, :], kpl_ref[rows, :], q_high, q_low)
+            q_ref[...] = q_own
         for copy in started:
             copy.wait_send()
+
+
+def finish(pre_ref, kph_ref, kpl_ref, q_ref, lam_ref, u_ref, lam_out):
+    u_ref[...] = pre_ref[...] - product(kph_ref[...], kpl_ref[...], q_ref[...])
+    lam_out[...] = lam_ref[...]
 
 
 def local(condensed, eigen_loads, coarse_inverse, face_rows, primal_rows, primal_slot):
@@ -290,25 +352,40 @@
     primal = primal_rows.shape[1]
     padded = 2 * width + -(-primal // LANES) * LANES
     outer, inner = grid_of(count)
-    slots = lax.broadcasted_iota(jnp.int32, (primal, primal), 0)
-    ordered = jnp.sum(jnp.where(primal_slot == slots, primal_rows, 0), axis=1)
-    fill = jnp.full((padded - 2 * width - primal,), -1, jnp.int32)
-    ids = jnp.concatenate([face_rows[0, 1], face_rows[0, 0], ordered, fill])[None]
+    corner_width = padded - 2 * width
     tile = 256 if order % 256 == 0 else order
     sends = (outer - 1) + (inner - 1) * outer + outer * inner
     dma = pltpu.SemaphoreType.DMA
     vmem = pl.BlockSpec(memory_space=pltpu.VMEM)
     face = pltpu.VMEM((ITERS, width, columns), F32)
     corner = pltpu.VMEM((width, padded - 2 * width), F32)
-    return pl.pallas_call(
+    smem = pl.BlockSpec(memory_space=pltpu.SMEM)
+    needed = 8 * order * (order + padded + 2 * columns) + 4 * padded * (order + columns + padded)
+    needed += 4 * owned * total * 8 + 4 * columns * (ITERS * (count * primal + 4 * width) + total)
+    needed += 4 * order * (columns + 2 * corner_width) + 4 * columns * (order + 8 * width)
+    shape = jax.ShapeDtypeStruct
+    held = [
+        pltpu.with_memory_space_constraint(value, pltpu.HBM)
+        for value in (face_rows, primal_rows, primal_slot, condensed, eigen_loads, coarse_inverse)
+    ]
+    parts = pl.pallas_call(
         functools.partial(kernel, count, primal, width),
         out_shape=(
-            jax.ShapeDtypeStruct((order, columns), F32),
-            jax.ShapeDtypeStruct((width, columns), F32),
+            shape((order, columns), F32),
+            shape((order, corner_width), BF16),
+            shape((order, corner_width), BF16),
+            shape((corner_width, columns), F32),
+            shape((width, columns), F32),
         ),
-        in_specs=[pl.BlockSpec(memory_space=pltpu.SMEM), vmem, pl.BlockSpec(memory_space=pl.ANY), vmem, vmem],
-        out_specs=(vmem, vmem),
+        in_specs=[smem, smem] + [pl.BlockSpec(memory_space=pltpu.HBM)] * 6,
+        out_specs=(vmem,) * 5,
         scratch_shapes=[
+            pltpu.VMEM(face_rows.shape, jnp.int32),
+            pltpu.VMEM(primal_rows.shape, jnp.int32),
+            pltpu.VMEM(primal_slot.shape, jnp.int32),
+            pltpu.VMEM((order, columns), F32),
+            pltpu.VMEM((owned, total), F32),
+            dma((5,)),
             pltpu.VMEM((order, order), F32),
             pltpu.VMEM((order, order), BF16),
             pltpu.VMEM((order, order), BF16),
@@ -316,21 +393,19 @@
             pltpu.VMEM((order, columns), BF16),
             pltpu.VMEM((order, columns), BF16),
             pltpu.VMEM((padded, order), F32),
+            pltpu.VMEM((padded, columns), F32),
             pltpu.VMEM((padded, padded), BF16),
             pltpu.VMEM((padded, padded), BF16),
             pltpu.VMEM((3, owned, total), F32),
             pltpu.VMEM((4 * owned, total), BF16),
             pltpu.VMEM((4 * owned, total), BF16),
-            pltpu.VMEM((order, padded - 2 * width), BF16),
-            pltpu.VMEM((order, padded - 2 * width), BF16),
-            pltpu.VMEM((order, columns), F32),
             pltpu.VMEM((ITERS, count, primal, columns), F32),
             pltpu.VMEM((total, columns), F32),
             face, face, face, face,
             corner, corner, corner, corner,
             dma((order // tile,)),
-            dma((ITERS, sends)),
-            dma((ITERS, count)),
+            dma((ITERS, 2 * sends)),
+            dma((ITERS, count, 2)),
             dma((2, ITERS, 2)),
             dma((3,)),
             dma((3,)),
@@ -338,9 +413,16 @@
             dma((2,)),
         ],
         compiler_params=pltpu.CompilerParams(
-            collective_id=0, has_side_effects=True, vmem_limit_bytes=67043328
+            collective_id=0, has_side_effects=True, vmem_limit_bytes=min(VMEM_LIMIT, needed + needed // 4)
         ),
-    )(ids, ids, condensed, eigen_loads, coarse_inverse)
+    )(face_rows, primal_rows, *held)
+    return pl.pallas_call(
+        finish,
+        out_shape=(shape((order, columns), F32), shape((width, columns), F32)),
+        in_specs=[vmem] * 5,
+        out_specs=(vmem, vmem),
+        compiler_params=pltpu.CompilerParams(vmem_limit_bytes=4 * order * columns * 8),
+    )(*parts)
 
 
 def solution(mesh):

time: 57.9 us -> 51.8 us (0.89); the launches traced: 57.7 us -> 51 us
  local copies, waits for them, and re-layouts: 4.87 us -> 0 us
  Pallas kernels: 51.3 us -> 50.4 us
  other arithmetic: 0.86 us -> 0 us
    unnamed x2 -> x0, local copies, waits for them, and re-layouts: 3.54 us -> none
    pallas_call x1, Pallas kernels: 51.3 us -> 49 us  [local(): pl.pallas_call(functools.partial(kernel, count, primal, width), out_shape...]
    pallas_call x0 -> x1, Pallas kernels: none -> 1.35 us  [local(): pl.pallas_call(finish, out_shape=(shape((order, columns), F32), shape((wi...]
    reduce_sum x1 -> x0, other arithmetic: 0.78 us -> none  [local(): ordered = jnp.sum(jnp.where(primal_slot == slots, primal_rows, 0), axis=1)]
    squeeze x1 -> x0, local copies, waits for them, and re-layouts: 0.77 us -> none  [local(): face_rows[0, 1]]
where the time goes in v2:
time: 51.8 us; the launch traced here: 51 us
  Pallas kernels  50.4 us (97%)
  between operations  0.64 us (1%)
    pallas_call x1, Pallas kernels, local(): pl.pallas_call(functools.partial(kernel, count, primal, width), out_shape...  49 us
    pallas_call x1, Pallas kernels, local(): pl.pallas_call(finish, out_shape=(shape((order, columns), F32), shape((wi...  1.35 us

profile of v2, /device:TPU:0, one launch (start us, length us, event | category | flops | bytes accessed | tf_op | source)
XLA Modules:
  0.0 51.0 jit_solution(9938959438042218805)
XLA Ops:
  0.6 49.0 %shard_map.77 = (f32[1536,128]{1,0:T(8,128)S(1)}, bf16[1536,128]{1,0:T(8,128)(2,1)S(1)}, bf16[1536,128]{1,0:T(8,128)(2,1)S(1)}, f32[128,128]{1,0:T(8,128)S(1)}, f32[128,128]{1,0:T(8,128)S(1)}) custom-call(s32[1,2,128]{2,1,0:T(2,128)} %face_hbm.1, s32[1,96]{1,0:T(1,128)} %prim_hbm.1, s32[1,2,128]{2,1,0:T(2,128)} %face_hbm.1, s32[1,96]{1,0:T(1,128)} %prim_hbm.1, ...), custom_call_target="tpu_custom_call" | custom-call | tf_op jit(solution)/shard_map/pallas_call | solution.py:371
  49.7 1.3 %shard_map.78 = (f32[1536,128]{1,0:T(8,128)}, f32[128,128]{1,0:T(8,128)}) custom-call(f32[1536,128]{1,0:T(8,128)S(1)} %get-tuple-element.7.pre_ref, bf16[1536,128]{1,0:T(8,128)(2,1)S(1)} %get-tuple-element.8.kph_ref, bf16[1536,128]{1,0:T(8,128)(2,1)S(1)} %get-tuple-element.9.kpl_ref, f32[128,128]{1,0:T(8,128)S(1)} %get-tuple-element.10.q_ref, ...), custom_call_target="tpu_custom_call" | custom-call | tf_op jit(solution)/shard_map/pallas_call | solution.py:419
